TPU v7x, 32 devices: a whole 2x2x4 slice. The times are simulated.
32 devices in a mesh: groups: 1, dp: 32 (over z, y, x, core).
Axes of the slice: x: 2, y: 2, z: 4, core: 2. Of those that a mesh axis runs over, the one named last changes fastest.
Arguments:
- activations: bfloat16 [128, 8192], P(('groups', 'dp')), may hold values from -6 to 6
- cotangent: bfloat16 [128, 8192], P(('groups', 'dp')), may hold values from -6 to 6
- w_gate: bfloat16 [28672, 8192], P('dp'), may hold values from -0.0625 to 0.0625
- w_up: bfloat16 [28672, 8192], P('dp'), may hold values from -0.0625 to 0.0625
- w_down: bfloat16 [28672, 8192], P('dp'), may hold values from -0.03125 to 0.03125
- proj_model: bfloat16 [8192, 192], P('dp'), may hold values from -0.0625 to 0.0625
- proj_hidden: bfloat16 [28672, 192], P('dp'), may hold values from -0.03125 to 0.03125
- seq_ids: int32 [128], P('groups'), may hold values from 0 to 15, never falling along the last dimension, each value on 1 to 16 neighbouring positions
- targets: bfloat16 [256, 3, 64, 64], P(('groups', 'dp')), may hold values from -24 to 24
- target_domain: int32 [256], P(('groups', 'dp')), may hold values from 0 to 31, never falling along the last dimension, each value on 1 to 16 neighbouring positions
Outputs:
- sketches: float32 [16, 3, 64, 64], P('groups')
- scores: float32 [16, 32], P('groups')
Inputs may be any that keep to these rules, and one draw needn't show every extreme that they name: `seq_ids`: never falling along the tokens; each of the 16 sequences has 1 to 16 tokens, one exactly 16. `target_domain`: never falling along the target examples; each of the 32 domains has 1 to 16 examples, one exactly 16.
All inputs are finite; a program needn't handle non-finite values.
Results may differ from a plain program's by a relative error of at most 0.0032.
Values may be sent and summed in bfloat16 or wider, within the bound.
A program may use at most 128 MiB of HBM per device.

v0:
```python
import jax
import jax.numpy as jnp
from jax import lax
from jax.sharding import PartitionSpec as P

DOMAINS = 32
SEQS = 16


def sequence_sketch(vectors, onehot, rank_size):
    blocks = vectors.reshape(vectors.shape[0], 6, rank_size)
    left_side = jnp.stack((blocks[:, 4], blocks[:, 5], blocks[:, 3]), 1)
    right_side = jnp.stack((blocks[:, 0], blocks[:, 1], blocks[:, 2]), 1)
    return jnp.einsum(
        "ns,nka,nkb->skab", onehot, left_side, right_side, precision=lax.Precision.HIGHEST
    )


def on_device(
    activations,
    cotangent,
    w_gate,
    w_up,
    w_down,
    proj_model,
    proj_hidden,
    seq_ids,
    targets,
    target_domain,
):
    rank_size = proj_model.shape[1] // 3
    model_cols = proj_model.shape[0]
    hidden_units = w_gate.shape[0]
    position = lax.axis_index("dp")
    offset = position * model_cols
    rows_in = lax.all_gather(activations, "dp", axis=0, tiled=True)
    gate_value = jnp.einsum("rd,fd->rf", rows_in, w_gate, preferred_element_type=jnp.float32)
    up_value = jnp.einsum("rd,fd->rf", rows_in, w_up, preferred_element_type=jnp.float32)
    columns = lax.dynamic_slice_in_dim(rows_in, offset, model_cols, 1)
    in_model = jnp.dot(columns, proj_model[:, : 2 * rank_size], preferred_element_type=jnp.float32)
    gate_value, up_value, in_model = (gate_value, up_value, in_model)
    forward_all = jnp.concatenate([gate_value, up_value, in_model], 1)
    gate_all = forward_all[:, :hidden_units]
    up_all = forward_all[:, hidden_units : 2 * hidden_units]
    in_model_all = forward_all[:, 2 * hidden_units :]
    gate_value = gate_all
    up_value = up_all
    rows_grad = lax.all_gather(cotangent, "dp", axis=0, tiled=True)
    sigmoid_gate = jax.nn.sigmoid(gate_value)
    silu_gate = gate_value * sigmoid_gate
    hidden = (silu_gate * up_value).astype(jnp.bfloat16)
    grad_hidden = jnp.einsum("rd,fd->rf", rows_grad, w_down, preferred_element_type=jnp.float32)
    grad_gate = (
        grad_hidden * up_value * sigmoid_gate * (1.0 + gate_value * (1.0 - sigmoid_gate))
    ).astype(jnp.bfloat16)
    grad_up = (grad_hidden * silu_gate).astype(jnp.bfloat16)
    columns = lax.dynamic_slice_in_dim(rows_grad, offset, model_cols, 1)
    out_down = jnp.dot(columns, proj_model[:, 2 * rank_size :], preferred_element_type=jnp.float32)
    in_down = jnp.dot(hidden, proj_hidden[:, :rank_size], preferred_element_type=jnp.float32)
    out_gate = jnp.dot(
        grad_gate, proj_hidden[:, rank_size : 2 * rank_size], preferred_element_type=jnp.float32
    )
    out_up = jnp.dot(grad_up, proj_hidden[:, 2 * rank_size :], preferred_element_type=jnp.float32)
    grads_all = jnp.concatenate([out_down, in_down, out_gate, out_up], 1)
    partials = jnp.concatenate([in_model_all, grads_all], 1)
    sequence_range = jnp.arange(SEQS)
    own_vectors = lax.psum_scatter(partials, "dp", scatter_dimension=0, tiled=True)
    own_count = own_vectors.shape[0]
    own_ids = lax.dynamic_slice_in_dim(seq_ids, position * own_count, own_count, 0)
    own_onehot = (own_ids[:, None] == sequence_range[None, :]).astype(jnp.float32)
    local_sketch = sequence_sketch(own_vectors, own_onehot, rank_size)
    sketches = lax.psum(local_sketch, "dp")
    entries = 3 * rank_size * rank_size
    flat_sketch = sketches.reshape(SEQS, entries)
    inverse_norm = lax.rsqrt(jnp.sum(flat_sketch * flat_sketch, 1) + 1e-06)
    domain_onehot = (target_domain[None, :] == jnp.arange(DOMAINS)[:, None]).astype(jnp.bfloat16)
    local_targets = targets.reshape(targets.shape[0], entries)
    domain_count = jnp.sum(domain_onehot.astype(jnp.float32), 1)
    target_products = jnp.dot(
        flat_sketch, local_targets.astype(jnp.float32).T, precision=lax.Precision.HIGHEST
    )
    folded = jnp.dot(
        target_products, domain_onehot.astype(jnp.float32).T, precision=lax.Precision.HIGHEST
    )
    total_scores, total_count = lax.psum((folded, domain_count), "dp")
    scores = total_scores / total_count[None, :] * inverse_norm[:, None]
    return (sketches, scores)


def solution(mesh):
    in_specs = (
        P(("groups", "dp"), None),
        P(("groups", "dp"), None),
        P("dp", None),
        P("dp", None),
        P("dp", None),
        P("dp", None),
        P("dp", None),
        P("groups"),
        P(("groups", "dp"), None, None, None),
        P(("groups", "dp")),
    )
    out_specs = (P("groups", None, None, None), P("groups", None))
    return jax.shard_map(
        on_device, mesh=mesh, in_specs=in_specs, out_specs=out_specs, check_vma=False
    )
```

profile of v0, /device:TPU:0, one launch (start us, length us, event | category | flops | bytes accessed | tf_op | source)
XLA Modules:
  0.0 479.7 jit_solution(16426818172373653184)
XLA Ops:
  7.2 0.0 copy-start
  7.2 0.0 all-gather.5.cloned.1.call-start
  7.2 0.7 all-gather.5.cloned.1.call-update
  7.9 0.0 all-gather.7.cloned.1.call-start
  8.0 0.7 all-gather.7.cloned.1.call-update
  8.7 0.0 all-reduce.7.cloned.1.call-start
  8.7 0.7 dynamic_slice.11
  9.4 0.0 copy-start.3
  9.4 60.4 %all-gather.5.cloned.1.call-done = bf16[32,4,8192]{2,1,0:T(4,128)(2,1)} async-done(((bf16[1,4,8192]{2,1,0:T(4,128)(2,1)}), bf16[32,4,8192]{2,1,0:T(4,128)(2,1)}) %all-gather.5.cloned.1.call-update) | async-done | bytes 2097168 | tf_op jit(solution)/shard_map/all_gather | solution.py:36
  69.8 2.5 reshape.18
  72.3 0.0 copy-done.3
  72.4 0.1 convolution_dynamic-update-slice_fusion
  72.5 55.3 %all-gather.7.cloned.1.call-done = bf16[32,4,8192]{2,1,0:T(4,128)(2,1)} async-done(((bf16[1,4,8192]{2,1,0:T(4,128)(2,1)}), bf16[32,4,8192]{2,1,0:T(4,128)(2,1)}) %all-gather.7.cloned.1.call-update) | async-done | bytes 2097168 | tf_op jit(solution)/shard_map/all_gather | solution.py:48
  127.7 3.9 reshape.20
  131.7 1.0 convolution_dynamic-update-slice_fusion.4
  132.6 10.6 %fusion.30 = f32[128,896]{1,0:T(8,128)S(1)} fusion(bf16[128,8192]{1,0:T(8,128)(2,1)} %reshape.20, bf16[896,8192]{1,0:T(8,128)(2,1)} %param.14), kind=kOutput, calls=%fused_computation.45 | convolution fusion | flops 1879048192 | bytes 17235968 | tf_op jit(solution)/shard_map/rd,fd->rf/dot_general | solution.py:52
  143.2 9.9 %fusion.28 = f32[128,896]{1,0:T(8,128)S(1)} fusion(bf16[128,8192]{1,0:T(8,128)(2,1)S(1)} %reshape.18, bf16[896,8192]{1,0:T(8,128)(2,1)} %param.12), kind=kOutput, calls=%fused_computation.43 | convolution fusion | flops 1879048192 | bytes 17235968 | tf_op jit(solution)/shard_map/rd,fd->rf/dot_general | solution.py:37
  153.1 0.0 copy-start.4
  153.1 9.9 %fusion.29 = f32[128,896]{1,0:T(8,128)S(1)} fusion(bf16[128,8192]{1,0:T(8,128)(2,1)S(1)} %reshape.18, bf16[896,8192]{1,0:T(8,128)(2,1)} %param.13), kind=kOutput, calls=%fused_computation.44 | convolution fusion | flops 1879048192 | bytes 17235968 | tf_op jit(solution)/shard_map/rd,fd->rf/dot_general | solution.py:38
  163.1 0.0 copy-done.4
  163.1 0.3 convolution_dynamic-update-slice_fusion.3
  163.4 0.3 convolution_dynamic-update-slice_fusion.2
  163.7 0.3 convolution_dynamic-update-slice_fusion.1
  164.0 0.0 copy-start.2
  164.0 0.0 copy-start.5
  164.0 0.7 copy-done.2
  164.7 0.0 all-reduce.7.cloned.1.call-update
  164.7 0.2 all-reduce.5.cloned.1.call-start
  165.0 123.5 %all-reduce.7.cloned.1.call-done = f32[128,384]{0,1:T(8,128)} async-done(((f32[128,384]{0,1:T(8,128)}), f32[128,384]{0,1:T(8,128)}) %all-reduce.7.cloned.1.call-update) | async-done | bytes 196624
  288.4 1.0 constant_dynamic-slice_fusion
  289.5 0.1 copy.37
  289.6 0.1 copy.24
  289.7 3.9 convolution_bitcast_fusion
  293.5 0.0 all-reduce.5.cloned.1.call-update
  293.6 0.0 copy-done.5
  293.6 0.1 convert_reduce_fusion
  293.6 134.0 %all-reduce.5.cloned.1.call-done = f32[16,3,64,64]{3,2,0,1:T(8,128)} async-done(((f32[16,3,64,64]{3,2,0,1:T(8,128)}), f32[16,3,64,64]{3,2,0,1:T(8,128)}) %all-reduce.5.cloned.1.call-update) | async-done | bytes 786448 | tf_op jit(solution)/shard_map/psum | solution.py:72
  427.6 0.0 copy-start.1
  427.6 1.8 multiply_reduce_fusion
  429.4 0.0 copy-done
  429.4 0.1 copy-done.1
  429.5 2.3 fusion.2
  431.8 0.2 fusion.21
  432.0 39.2 %all-reduce.1 = (f32[16,32]{1,0:T(8,128)S(1)}, f32[32]{0:T(128)S(1)}) all-reduce(f32[16,32]{1,0:T(8,128)S(1)} %fusion.21, f32[32]{0:T(128)S(1)} %convert_reduce_fusion), channel_id=1, replica_groups=mesh['groups'=1,'dp'=32] {'dp'}, use_global_device_ids=true, to_apply=%region_2.0 | all-reduce | flops 544 | bytes 4352 | tf_op jit(solution)/shard_map/psum | solution.py:85
  471.3 0.7 divide_multiply_fusion
  471.9 1.2 copy.29
  (5 shorter events, 0.0 us)
Async XLA Ops:
  7.2 422.3 %copy-start = (bf16[8,3,64,64]{3,2,1,0:T(8,128)(2,1)S(1)}, bf16[8,3,64,64]{3,2,1,0:T(8,128)(2,1)}, u32[]{:S(2)}) copy-start(bf16[8,3,64,64]{3,2,1,0:T(8,128)(2,1)} %param.18) | copy-start | bytes 589828
  7.2 62.6 %all-gather.5.cloned.1.call-start = ((), (), s32[]{:S(2)}) async-start(), calls=%async_computation.1 | async-start | bytes 2162688 | tf_op jit(solution)/shard_map/all_gather | solution.py:36
  7.9 119.8 %all-gather.7.cloned.1.call-start = ((), (), s32[]{:S(2)}) async-start(), calls=%async_computation.2 | async-start | bytes 2162688 | tf_op jit(solution)/shard_map/all_gather | solution.py:48
  8.7 279.8 %all-reduce.7.cloned.1.call-start = ((), (), s32[]{:S(2)}) async-start(), calls=%async_computation.3 | async-start | bytes 393216
  9.4 62.9 %copy-start.3 = (bf16[256,192]{0,1:T(8,128)(2,1)S(1)}, bf16[256,192]{0,1:T(8,128)(2,1)}, u32[]{:S(2)}) copy-start(bf16[256,192]{0,1:T(8,128)(2,1)} %param.15) | copy-start | bytes 294916
  153.1 10.0 %copy-start.4 = (bf16[896,192]{0,1:T(8,128)(2,1)S(1)}, bf16[896,192]{0,1:T(8,128)(2,1)}, u32[]{:S(2)}) copy-start(bf16[896,192]{0,1:T(8,128)(2,1)} %param.16) | copy-start | bytes 1032196
  164.0 0.7 copy-start.2
  164.0 129.5 %copy-start.5 = (s32[8]{0:T(128)S(1)}, s32[8]{0:T(128)}, u32[]{:S(2)}) copy-start(s32[8]{0:T(128)} %param.19) | copy-start | bytes 100
  164.7 262.9 %all-reduce.5.cloned.1.call-start = ((), (), s32[]{:S(2)}) async-start(), calls=%async_computation | async-start | bytes 3145728 | tf_op jit(solution)/shard_map/psum | solution.py:72
  427.6 1.9 copy-start.1
Sparse Core Ops, SparseCore 0:
  10.8 58.9 all-gather.4
  72.7 55.0 all-gather.6
  164.8 123.5 all-reduce.6
  294.1 133.4 all-reduce.4
where the time goes:
time: 480 us
  waiting for transfers between devices  374 us (78%)
  blocking collectives  39.2 us (8%)
  matrix products  38.8 us (8%)
  between operations  13.9 us (3%)
  local copies, waits for them, and re-layouts  10.4 us (2%)
    psum x1, waiting for transfers between devices, on_device(): sketches = lax.psum(local_sketch, 'dp')  134 us
    unnamed x5, waiting for transfers between devices  125 us
    all_gather x1, waiting for transfers between devices, on_device(): rows_in = lax.all_gather(activations, 'dp', axis=0, tiled=True)  60.4 us
    all_gather x1, waiting for transfers between devices, on_device(): rows_grad = lax.all_gather(cotangent, 'dp', axis=0, tiled=True)  55.3 us
    psum x1, blocking collectives, on_device(): total_scores, total_count = lax.psum((folded, domain_count), 'dp')  39.2 us
    dot_general x1, matrix products, on_device(): jnp.einsum('rd,fd->rf', rows_grad, w_down, preferred_element_type=jnp.flo...  10.6 us
    dot_general x1, matrix products, on_device(): jnp.einsum('rd,fd->rf', rows_in, w_up, preferred_element_type=jnp.float32)  9.95 us
    dot_general x1, matrix products, on_device(): jnp.einsum('rd,fd->rf', rows_in, w_gate, preferred_element_type=jnp.float32)  9.9 us
  transfers between devices with their start and end apart: 4, of which 4 were waited for; matrix products, arithmetic and copies ran while one was open for 1% of the time, Pallas kernels for 0%

commit v1 on v0

--- a/solution.py
+++ b/solution.py
@@ -69,7 +69,11 @@
     own_ids = lax.dynamic_slice_in_dim(seq_ids, position * own_count, own_count, 0)
     own_onehot = (own_ids[:, None] == sequence_range[None, :]).astype(jnp.float32)
     local_sketch = sequence_sketch(own_vectors, own_onehot, rank_size)
-    sketches = lax.psum(local_sketch, "dp")
+    n_dev = lax.axis_size("dp")
+    sketches, reach = (local_sketch, 1)
+    while reach < n_dev:
+        sketches = sketches + lax.ppermute(sketches, "dp", [(i, i ^ reach) for i in range(n_dev)])
+        reach = 2 * reach
     entries = 3 * rank_size * rank_size
     flat_sketch = sketches.reshape(SEQS, entries)
     inverse_norm = lax.rsqrt(jnp.sum(flat_sketch * flat_sketch, 1) + 1e-06)

time: 480 us -> 524 us (1.092)
  waiting for transfers between devices: 374 us -> 413 us
  starting transfers between devices: 0.34 us -> 8.47 us
    ppermute x0 -> x5, waiting for transfers between devices: none -> 172 us  [on_device(): lax.ppermute(sketches, 'dp', [(i, i ^ reach) for i in range(n_dev)])]
    psum x1 -> x0, waiting for transfers between devices: 134 us -> none  [on_device(): sketches = lax.psum(local_sketch, 'dp')]
    ppermute x0 -> x5, starting transfers between devices: none -> 8.36 us  [on_device(): lax.ppermute(sketches, 'dp', [(i, i ^ reach) for i in range(n_dev)])]
    unnamed x5 -> x4, waiting for transfers between devices: 125 us -> 125 us
  transfers between devices with their start and end apart: 4 -> 8, of which waited for: 4 -> 8; matrix products, arithmetic and copies ran while one was open for 1% -> 1% of each run, Pallas kernels for 0% -> 0%
where the time goes in v1:
time: 524 us
  waiting for transfers between devices  413 us (79%)
  matrix products  37.8 us (7%)
  blocking collectives  37.8 us (7%)
  between operations  13.9 us (3%)
  local copies, waits for them, and re-layouts  10.4 us (2%)
  starting transfers between devices  8.47 us (2%)
    ppermute x5, waiting for transfers between devices, on_device(): lax.ppermute(sketches, 'dp', [(i, i ^ reach) for i in range(n_dev)])  172 us
    unnamed x4, waiting for transfers between devices  125 us
    all_gather x1, waiting for transfers between devices, on_device(): rows_in = lax.all_gather(activations, 'dp', axis=0, tiled=True)  60.4 us
    all_gather x1, waiting for transfers between devices, on_device(): rows_grad = lax.all_gather(cotangent, 'dp', axis=0, tiled=True)  55.3 us
    psum x1, blocking collectives, on_device(): total_scores, total_count = lax.psum((folded, domain_count), 'dp')  37.8 us
    dot_general x1, matrix products, on_device(): jnp.einsum('rd,fd->rf', rows_grad, w_down, preferred_element_type=jnp.flo...  10.6 us
  transfers between devices with their start and end apart: 8, of which 8 were waited for; matrix products, arithmetic and copies ran while one was open for 1% of the time, Pallas kernels for 0%

profile of v1, /device:TPU:0, one launch (start us, length us, event | category | flops | bytes accessed | tf_op | source)
XLA Modules:
  0.0 524.0 jit_solution(16730474176641072675)
XLA Ops:
  7.2 0.0 copy-start
  7.2 0.0 all-gather.5.cloned.1.call-start
  7.2 0.7 all-gather.5.cloned.1.call-update
  7.9 0.0 all-gather.7.cloned.1.call-start
  8.0 0.7 all-gather.7.cloned.1.call-update
  8.7 0.0 all-reduce.4.cloned.1.call-start
  8.7 0.7 dynamic_slice.11
  9.4 0.0 copy-start.2
  9.4 60.4 %all-gather.5.cloned.1.call-done = bf16[32,4,8192]{2,1,0:T(4,128)(2,1)} async-done(((bf16[1,4,8192]{2,1,0:T(4,128)(2,1)}), bf16[32,4,8192]{2,1,0:T(4,128)(2,1)}) %all-gather.5.cloned.1.call-update) | async-done | bytes 2097168 | tf_op jit(solution)/shard_map/all_gather | solution.py:36
  69.8 2.5 reshape.18
  72.3 0.0 copy-done.2
  72.4 0.1 convolution_dynamic-update-slice_fusion
  72.5 55.3 %all-gather.7.cloned.1.call-done = bf16[32,4,8192]{2,1,0:T(4,128)(2,1)} async-done(((bf16[1,4,8192]{2,1,0:T(4,128)(2,1)}), bf16[32,4,8192]{2,1,0:T(4,128)(2,1)}) %all-gather.7.cloned.1.call-update) | async-done | bytes 2097168 | tf_op jit(solution)/shard_map/all_gather | solution.py:48
  127.7 4.0 reshape.20
  131.7 1.0 convolution_dynamic-update-slice_fusion.4
  132.7 10.6 %fusion.30 = f32[128,896]{1,0:T(8,128)S(1)} fusion(bf16[128,8192]{1,0:T(8,128)(2,1)} %reshape.20, bf16[896,8192]{1,0:T(8,128)(2,1)} %param.14), kind=kOutput, calls=%fused_computation.45 | convolution fusion | flops 1879048192 | bytes 17235968 | tf_op jit(solution)/shard_map/rd,fd->rf/dot_general | solution.py:52
  143.2 9.9 %fusion.28 = f32[128,896]{1,0:T(8,128)S(1)} fusion(bf16[128,8192]{1,0:T(8,128)(2,1)S(1)} %reshape.18, bf16[896,8192]{1,0:T(8,128)(2,1)} %param.12), kind=kOutput, calls=%fused_computation.43 | convolution fusion | flops 1879048192 | bytes 17235968 | tf_op jit(solution)/shard_map/rd,fd->rf/dot_general | solution.py:37
  153.2 0.0 copy-start.3
  153.2 9.9 %fusion.29 = f32[128,896]{1,0:T(8,128)S(1)} fusion(bf16[128,8192]{1,0:T(8,128)(2,1)S(1)} %reshape.18, bf16[896,8192]{1,0:T(8,128)(2,1)} %param.13), kind=kOutput, calls=%fused_computation.44 | convolution fusion | flops 1879048192 | bytes 17235968 | tf_op jit(solution)/shard_map/rd,fd->rf/dot_general | solution.py:38
  163.1 0.0 copy-done.3
  163.1 0.3 convolution_dynamic-update-slice_fusion.3
  163.4 0.3 convolution_dynamic-update-slice_fusion.2
  163.7 0.3 convolution_dynamic-update-slice_fusion.1
  164.0 0.0 copy-start.1
  164.0 0.7 copy-done.1
  164.7 0.0 all-reduce.4.cloned.1.call-update
  164.7 123.6 %all-reduce.4.cloned.1.call-done = f32[128,384]{0,1:T(8,128)} async-done(((f32[128,384]{0,1:T(8,128)}), f32[128,384]{0,1:T(8,128)}) %all-reduce.4.cloned.1.call-update) | async-done | bytes 196624
  288.4 1.0 constant_dynamic-slice_fusion
  289.5 0.1 copy.37
  289.5 0.1 copy.24
  289.6 2.9 convolution_bitcast_fusion
  292.5 0.1 collective-permute-start
  292.6 3.4 collective-permute-done
  296.0 0.4 add.45
  296.4 1.5 collective-permute-start.1
  297.9 35.0 %collective-permute-done.1 = f32[16,3,64,64]{3,2,0,1:T(8,128)S(1)} collective-permute-done((f32[16,3,64,64]{3,2,0,1:T(8,128)S(1)}, f32[16,3,64,64]{3,2,0,1:T(8,128)S(1)}, u32[]{:S(2)}, u32[]{:S(2)}) %collective-permute-start.1) | collective-permute-done | bytes 786464 | tf_op jit(solution)/shard_map/ppermute | solution.py:75
  332.9 0.4 add.46
  333.2 1.5 collective-permute-start.2
  334.8 34.1 %collective-permute-done.2 = f32[16,3,64,64]{3,2,0,1:T(8,128)S(1)} collective-permute-done((f32[16,3,64,64]{3,2,0,1:T(8,128)S(1)}, f32[16,3,64,64]{3,2,0,1:T(8,128)S(1)}, u32[]{:S(2)}, u32[]{:S(2)}) %collective-permute-start.2) | collective-permute-done | bytes 786464 | tf_op jit(solution)/shard_map/ppermute | solution.py:75
  368.9 0.4 add.47
  369.2 0.0 copy-start.4
  369.2 3.4 collective-permute-start.3
  372.7 33.0 %collective-permute-done.3 = f32[16,3,64,64]{3,2,0,1:T(8,128)S(1)} collective-permute-done((f32[16,3,64,64]{3,2,0,1:T(8,128)S(1)}, f32[16,3,64,64]{3,2,0,1:T(8,128)S(1)}, u32[]{:S(2)}, u32[]{:S(2)}) %collective-permute-start.3) | collective-permute-done | bytes 786464 | tf_op jit(solution)/shard_map/ppermute | solution.py:75
  405.6 0.4 add.48
  406.0 1.8 collective-permute-start.4
  407.8 0.0 copy-done.4
  407.8 0.1 convert_reduce_fusion
  407.9 66.9 %collective-permute-done.4 = f32[16,3,64,64]{3,2,0,1:T(8,128)S(1)} collective-permute-done((f32[16,3,64,64]{3,2,0,1:T(8,128)S(1)}, f32[16,3,64,64]{3,2,0,1:T(8,128)S(1)}, u32[]{:S(2)}, u32[]{:S(2)}) %collective-permute-start.4) | collective-permute-done | bytes 786464 | tf_op jit(solution)/shard_map/ppermute | solution.py:75
  474.8 0.4 multiply_reduce_fusion
  475.3 1.3 copy.29
  476.5 0.0 copy-done
  476.5 2.3 fusion.2
  478.8 0.2 fusion.21
  479.1 37.8 %all-reduce.1 = (f32[16,32]{1,0:T(8,128)S(1)}, f32[32]{0:T(128)S(1)}) all-reduce(f32[16,32]{1,0:T(8,128)S(1)} %fusion.21, f32[32]{0:T(128)S(1)} %convert_reduce_fusion), channel_id=1, replica_groups=mesh['groups'=1,'dp'=32] {'dp'}, use_global_device_ids=true, to_apply=%region_1.0 | all-reduce | flops 544 | bytes 4352 | tf_op jit(solution)/shard_map/psum | solution.py:89
  516.8 0.7 divide_multiply_fusion
  (5 shorter events, 0.0 us)
Async XLA Ops:
  7.2 469.4 %copy-start = (bf16[8,3,64,64]{3,2,1,0:T(8,128)(2,1)S(1)}, bf16[8,3,64,64]{3,2,1,0:T(8,128)(2,1)}, u32[]{:S(2)}) copy-start(bf16[8,3,64,64]{3,2,1,0:T(8,128)(2,1)} %param.18) | copy-start | bytes 589828
  7.2 62.6 %all-gather.5.cloned.1.call-start = ((), (), s32[]{:S(2)}) async-start(), calls=%async_computation | async-start | bytes 2162688 | tf_op jit(solution)/shard_map/all_gather | solution.py:36
  7.9 119.8 %all-gather.7.cloned.1.call-start = ((), (), s32[]{:S(2)}) async-start(), calls=%async_computation.1 | async-start | bytes 2162688 | tf_op jit(solution)/shard_map/all_gather | solution.py:48
  8.7 279.7 %all-reduce.4.cloned.1.call-start = ((), (), s32[]{:S(2)}) async-start(), calls=%async_computation.2 | async-start | bytes 393216
  9.4 62.9 %copy-start.2 = (bf16[256,192]{0,1:T(8,128)(2,1)S(1)}, bf16[256,192]{0,1:T(8,128)(2,1)}, u32[]{:S(2)}) copy-start(bf16[256,192]{0,1:T(8,128)(2,1)} %param.15) | copy-start | bytes 294916
  153.2 10.0 %copy-start.3 = (bf16[896,192]{0,1:T(8,128)(2,1)S(1)}, bf16[896,192]{0,1:T(8,128)(2,1)}, u32[]{:S(2)}) copy-start(bf16[896,192]{0,1:T(8,128)(2,1)} %param.16) | copy-start | bytes 1032196
  164.0 0.7 copy-start.1
  292.5 3.5 collective-permute-start
  296.4 36.5 %collective-permute-start.1 = (f32[16,3,64,64]{3,2,0,1:T(8,128)S(1)}, f32[16,3,64,64]{3,2,0,1:T(8,128)S(1)}, u32[]{:S(2)}, u32[]{:S(2)}) collective-permute-start(f32[16,3,64,64]{3,2,0,1:T(8,128)S(1)} %add.45), channel_id=1, source_target_pairs={{0,2},{1,3},{2,0},{3,1},{4,6},{5,7},{6,4},{7,5},{8,10},{9,11},{10,... | collective-permute-start | bytes 2359304 | tf_op jit(solution)/shard_map/ppermute | solution.py:75
  333.2 35.6 %collective-permute-start.2 = (f32[16,3,64,64]{3,2,0,1:T(8,128)S(1)}, f32[16,3,64,64]{3,2,0,1:T(8,128)S(1)}, u32[]{:S(2)}, u32[]{:S(2)}) collective-permute-start(f32[16,3,64,64]{3,2,0,1:T(8,128)S(1)} %add.46), channel_id=1, source_target_pairs={{0,4},{1,5},{2,6},{3,7},{4,0},{5,1},{6,2},{7,3},{8,12},{9,13},{10,... | collective-permute-start | bytes 2359304 | tf_op jit(solution)/shard_map/ppermute | solution.py:75
  369.2 38.6 %copy-start.4 = (s32[8]{0:T(128)S(1)}, s32[8]{0:T(128)}, u32[]{:S(2)}) copy-start(s32[8]{0:T(128)} %param.19) | copy-start | bytes 100
  369.2 36.4 %collective-permute-start.3 = (f32[16,3,64,64]{3,2,0,1:T(8,128)S(1)}, f32[16,3,64,64]{3,2,0,1:T(8,128)S(1)}, u32[]{:S(2)}, u32[]{:S(2)}) collective-permute-start(f32[16,3,64,64]{3,2,0,1:T(8,128)S(1)} %add.47), channel_id=1, source_target_pairs={{0,8},{1,9},{2,10},{3,11},{4,12},{5,13},{6,14},{7,15},{8,0},{9,1},... | collective-permute-start | bytes 2359304 | tf_op jit(solution)/shard_map/ppermute | solution.py:75
  406.0 68.8 %collective-permute-start.4 = (f32[16,3,64,64]{3,2,0,1:T(8,128)S(1)}, f32[16,3,64,64]{3,2,0,1:T(8,128)S(1)}, u32[]{:S(2)}, u32[]{:S(2)}) collective-permute-start(f32[16,3,64,64]{3,2,0,1:T(8,128)S(1)} %add.48), channel_id=1, source_target_pairs={{0,16},{1,17},{2,18},{3,19},{4,20},{5,21},{6,22},{7,23},{8,24},{9,... | collective-permute-start | bytes 2359304 | tf_op jit(solution)/shard_map/ppermute | solution.py:75
Sparse Core Ops, SparseCore 0:
  10.8 58.9 all-gather.4
  72.7 55.0 all-gather.6
  164.8 123.5 all-reduce.3
